TPU v7x, 32 devices: a whole 2x2x4 slice. The times are simulated.
32 devices in a mesh: section: 4 (over x, core), dp: 2 (over y), ctx: 4 (over z).
Axes of the slice: x: 2, y: 2, z: 4, core: 2. Of those that a mesh axis runs over, the one named last changes fastest.
Arguments:
- layer_input: bfloat16 [4, 2, 512, 4096], P('section', 'dp', 'ctx'), may hold values from -6 to 6
- attn_grad: bfloat16 [4, 2, 512, 4096], P('section', 'dp', 'ctx'), may hold values from -48 to 48
- queries: bfloat16 [4, 2, 512, 4096], P('section', 'dp', None, 'ctx'), may hold values from -6 to 6
- keys: bfloat16 [4, 2, 512, 512], P('section', 'dp', 'ctx'), may hold values from -6 to 6
- values: bfloat16 [4, 2, 512, 512], P('section', 'dp', 'ctx'), may hold values from -4 to 4
- kv_weight: bfloat16 [4, 4096, 1024], P('section', 'ctx'), may hold values from -0.09375 to 0.09375
- segments: int32 [2, 512], P('dp'), may hold values from 0 to 3, as said below
- positions: int32 [2, 512], P('dp'), may hold values from 0 to 16383, as said below
Outputs:
- grad_prev: bfloat16 [4, 2, 512, 4096], P('section', 'dp', 'ctx')
- query_grad: bfloat16 [4, 2, 512, 4096], P('section', 'dp', 'ctx')
- weight_grad: float32 [4, 4096, 1024], P('section', 'ctx', 'dp')
Inputs may be any that keep to these rules, and one draw needn't show every extreme that they name: `segments`: every sequence holds four documents: segment ids start at 0, never fall, and end at 3. Inside a segment positions rise by one a token.
All inputs are finite; a program needn't handle non-finite values.
Results may differ from a plain program's by a relative error of at most 0.012.
Values may be sent and summed in bfloat16 or wider, within the bound.
No kernel may reach another device: no remote copies, remote signals or barrier semaphores. Data moves between devices by JAX's collectives and lax.ppermute only.
A program may use at most 128 MiB of HBM per device.

v0:
```python
import math
import jax
import jax.numpy as jnp
import numpy as np
from jax import lax
from jax.sharding import PartitionSpec as P

QUERY_HEADS = 32
KEY_VALUE_HEADS = 4
HEAD_WIDTH = 128


def passed_along(value, axis, by):
    size = lax.axis_size(axis)
    pairs = [(i, i + by) for i in range(size) if 0 <= i + by < size]
    return lax.ppermute(value, axis, pairs)


def yarn_table(head_size):
    theta_base = 1000000.0
    factor = 4.0
    pretrain_len = 32768.0
    exponent = np.arange(0, head_size, 2) / head_size
    extrapolated = 1.0 / theta_base**exponent
    interpolated = extrapolated / factor

    def boundary(rotations):
        return (
            head_size
            * math.log(pretrain_len / (rotations * 2.0 * math.pi))
            / (2.0 * math.log(theta_base))
        )

    lower_dim = max(math.floor(boundary(32.0)), 0)
    upper_dim = min(math.ceil(boundary(1.0)), head_size - 1)
    ramp_width = max(upper_dim - lower_dim, 0.001)
    ramp_share = np.clip((np.arange(head_size // 2) - lower_dim) / ramp_width, 0.0, 1.0)
    keep_share = 1.0 - ramp_share
    frequency = interpolated * (1.0 - keep_share) + extrapolated * keep_share
    return (frequency.astype(np.float32), float(0.1 * math.log(factor) + 1.0))


def rotate_back(gradient, places, frequency, mscale):
    angles = places.astype(jnp.float32)[:, None] * frequency[None, :]
    cosine = jnp.cos(angles) * mscale
    sine_term = jnp.sin(angles) * mscale
    cosine = jnp.concatenate([cosine, cosine], -1)[:, None, :]
    sine_term = jnp.concatenate([sine_term, sine_term], -1)[:, None, :]
    half_size = gradient.shape[-1] // 2
    turned = jnp.concatenate([gradient[..., half_size:], -gradient[..., :half_size]], -1)
    return gradient * cosine + turned * sine_term


def attend_local(query_heads, key_heads, value_heads, grad_heads, seg_ids):
    sequence_length = query_heads.shape[0]
    local_heads = query_heads.shape[1] // HEAD_WIDTH
    kv_heads = key_heads.shape[1] // HEAD_WIDTH
    group_share_count = local_heads // kv_heads
    score_scale = HEAD_WIDTH ** (-0.5)
    query_complete = query_heads.reshape(sequence_length, kv_heads, group_share_count, HEAD_WIDTH)
    key_complete = key_heads.reshape(sequence_length, kv_heads, HEAD_WIDTH)
    value_complete = value_heads.reshape(sequence_length, kv_heads, HEAD_WIDTH)
    gradient_total = grad_heads.reshape(sequence_length, kv_heads, group_share_count, HEAD_WIDTH)
    block_rows = min(512, sequence_length)
    dq_parts = []
    key_gradient = jnp.zeros((sequence_length, kv_heads, HEAD_WIDTH), jnp.float32)
    value_gradient = jnp.zeros((sequence_length, kv_heads, HEAD_WIDTH), jnp.float32)
    for block_index in range(sequence_length // block_rows):
        row_start = block_index * block_rows
        row_stop = row_start + block_rows
        q_blk = query_complete[row_start:row_stop]
        k_blk = key_complete[:row_stop]
        v_blk = value_complete[:row_stop]
        g_blk = gradient_total[row_start:row_stop]
        scores = (
            jnp.einsum("qkgd,lkd->kgql", q_blk, k_blk, preferred_element_type=jnp.float32)
            * score_scale
        )
        row_ids = jnp.arange(row_start, row_stop)[:, None]
        col_ids = jnp.arange(row_stop)[None, :]
        allowed = (col_ids <= row_ids) & (
            seg_ids[row_start:row_stop][:, None] == seg_ids[:row_stop][None, :]
        )
        scores = jnp.where(allowed, scores, -1e30)
        row_max = jnp.max(scores, -1, keepdims=True)
        shifted = jnp.exp(scores - row_max)
        row_total = jnp.sum(shifted, -1, keepdims=True)
        attention = shifted / row_total
        probs_half = attention.astype(jnp.bfloat16)
        outputs = jnp.einsum(
            "kgql,lkd->qkgd", probs_half, v_blk, preferred_element_type=jnp.float32
        )
        row_delta = jnp.transpose(jnp.sum(g_blk.astype(jnp.float32) * outputs, -1), (1, 2, 0))[
            ..., None
        ]
        dprobs = jnp.einsum("qkgd,lkd->kgql", g_blk, v_blk, preferred_element_type=jnp.float32)
        dscore_half = (attention * (dprobs - row_delta)).astype(jnp.bfloat16)
        dq_parts.append(
            jnp.einsum("kgql,lkd->qkgd", dscore_half, k_blk, preferred_element_type=jnp.float32)
            * score_scale
        )
        key_gradient = key_gradient.at[:row_stop].add(
            jnp.einsum("kgql,qkgd->lkd", dscore_half, q_blk, preferred_element_type=jnp.float32)
            * score_scale
        )
        value_gradient = value_gradient.at[:row_stop].add(
            jnp.einsum("kgql,qkgd->lkd", probs_half, g_blk, preferred_element_type=jnp.float32)
        )
    query_grad = jnp.concatenate(dq_parts, 0).reshape(sequence_length, local_heads, HEAD_WIDTH)
    return (query_grad, key_gradient, value_gradient)


def on_device(layer_input, attn_grad, queries, keys, values, kv_weight, segments, positions):
    frequency, mscale = yarn_table(HEAD_WIDTH)
    inputs = layer_input[0, 0]
    output_gradient = attn_grad[0, 0]
    query_heads = queries[0, 0]
    key_row_block = keys[0, 0]
    value_row_block = values[0, 0]
    weight_rows = kv_weight[0]
    seg_ids = segments[0]
    places = positions[0]
    ctx_size = lax.axis_size("ctx")
    ctx_index = lax.axis_index("ctx")
    data_size = lax.axis_size("dp")
    sequence_length = query_heads.shape[0]
    kv_width = key_row_block.shape[1]
    kv_heads = kv_width // HEAD_WIDTH
    local_heads = query_heads.shape[1] // HEAD_WIDTH
    group_share_count = QUERY_HEADS // KEY_VALUE_HEADS
    kv_local = max(1, kv_heads // ctx_size)
    grad_heads = lax.all_to_all(output_gradient, "ctx", split_axis=1, concat_axis=0, tiled=True)
    key_complete, value_complete = (
        lax.all_gather(key_row_block, "ctx", axis=0, tiled=True),
        lax.all_gather(value_row_block, "ctx", axis=0, tiled=True),
    )
    first_col = ctx_index * local_heads // group_share_count * HEAD_WIDTH
    key_heads = lax.dynamic_slice_in_dim(key_complete, first_col, kv_local * HEAD_WIDTH, 1)
    value_heads = lax.dynamic_slice_in_dim(value_complete, first_col, kv_local * HEAD_WIDTH, 1)
    query_grad, key_gradient, value_gradient = attend_local(
        query_heads, key_heads, value_heads, grad_heads, seg_ids
    )
    query_back = (
        rotate_back(query_grad, places, frequency, mscale)
        .astype(jnp.bfloat16)
        .reshape(sequence_length, local_heads * HEAD_WIDTH)
    )
    query_out = lax.all_to_all(query_back, "ctx", split_axis=0, concat_axis=1, tiled=True)
    key_back = rotate_back(key_gradient, places, frequency, mscale).reshape(
        sequence_length, kv_local * HEAD_WIDTH
    )
    value_back = value_gradient.reshape(sequence_length, kv_local * HEAD_WIDTH)
    zeros_full = jnp.zeros((sequence_length, kv_width), jnp.float32)
    key_full = lax.dynamic_update_slice_in_dim(zeros_full, key_back, first_col, 1)
    value_full = lax.dynamic_update_slice_in_dim(zeros_full, value_back, first_col, 1)
    key_sum, value_sum = (
        lax.psum_scatter(key_full, "ctx", scatter_dimension=0, tiled=True),
        lax.psum_scatter(value_full, "ctx", scatter_dimension=0, tiled=True),
    )
    kv_grad = jnp.concatenate([key_sum, value_sum], 1).astype(jnp.bfloat16)
    input_cols = lax.all_to_all(inputs, "ctx", split_axis=1, concat_axis=0, tiled=True)
    gradient_total = lax.all_gather(kv_grad, "ctx", axis=0, tiled=True)
    rows_part = jnp.einsum(
        "td,tc->dc", input_cols, gradient_total, preferred_element_type=jnp.float32
    )
    cols_back = jnp.einsum(
        "tc,rc->tr", gradient_total, weight_rows, preferred_element_type=jnp.float32
    ).astype(jnp.bfloat16)
    back_rows = lax.all_to_all(cols_back, "ctx", split_axis=0, concat_axis=1, tiled=True)
    weight_grad = lax.psum_scatter(rows_part, "dp", scatter_dimension=1, tiled=True) / data_size
    grad_prev = passed_along(back_rows, "section", -1)
    return (grad_prev[None, None], query_out[None, None], weight_grad[None])


def solution(mesh):
    return jax.shard_map(
        on_device,
        mesh=mesh,
        in_specs=(
            P("section", "dp", "ctx", None),
            P("section", "dp", "ctx", None),
            P("section", "dp", None, "ctx"),
            P("section", "dp", "ctx", None),
            P("section", "dp", "ctx", None),
            P("section", "ctx", None),
            P("dp", None),
            P("dp", None),
        ),
        out_specs=(
            P("section", "dp", "ctx", None),
            P("section", "dp", "ctx", None),
            P("section", "ctx", "dp"),
        ),
        check_vma=False,
    )
```

profile of v0, /device:TPU:0, one launch (start us, length us, event | category | flops | bytes accessed | tf_op | source)
XLA Modules:
  0.0 270.1 jit_solution(15797264139231069279)
XLA Ops:
  10.5 6.3 %all-to-all-start = ((bf16[128,4,1024]{2,0,1:T(8,128)(2,1)}), bf16[128,4,1024]{2,0,1:T(8,128)(2,1)S(1)}, u32[]{:S(2)}, u32[]{:S(2)}) async-start(bf16[128,4,1024]{2,0,1:T(8,128)(2,1)} %copy.78), calls=%async_computation | async-start | bytes 2097152 | tf_op jit(solution)/shard_map/all_to_all | solution.py:132
  19.1 34.3 %all-gather = bf16[1,1,512,512]{3,2,1,0:T(8,128)(2,1)} all-gather(bf16[1,1,128,512]{3,2,1,0:T(8,128)(2,1)S(1)} %copy-done.10), channel_id=2, replica_groups=mesh['section'=4,'dp'=2,'ctx'=4] {'ctx'}, dimensions={2}, use_global_device_ids=true | all-gather | bytes 655360 | tf_op jit(solution)/shard_map/all_gather | solution.py:134
  53.4 16.6 %all-gather.1 = bf16[1,1,512,512]{3,2,1,0:T(8,128)(2,1)} all-gather(bf16[1,1,128,512]{3,2,1,0:T(8,128)(2,1)S(1)} %copy-done.11), channel_id=3, replica_groups=mesh['section'=4,'dp'=2,'ctx'=4] {'ctx'}, dimensions={2}, use_global_device_ids=true | all-gather | bytes 655360 | tf_op jit(solution)/shard_map/all_gather | solution.py:135
  71.5 2.8 %fusion.4 = (f32[8,512]{1,0:T(8,128)S(1)}, f32[512,512,8]{1,0,2:T(8,128)S(1)}) fusion(pred[512,512]{0,1:T(8,128)(4,1)S(1)} %fusion.27, bf16[512,8,128]{0,2,1:T(8,128)(2,1)} %bitcast.156, bf16[1,1,512,512]{3,2,1,0:T(8,128)(2,1)} %all-gather, s32[]{:T(128)S(6)} %select_n.16), kind=kOutput, calls=%fused_computation.7 | convolution fusion | flops 543158272 | bytes 9846788 | tf_op jit(solution)/shard_map/qkgd,lkd->kgql/dot_general | solution.py:76
  74.4 3.3 %copy-done.1 = f32[512,512,8]{1,0,2:T(8,128)} copy-done((f32[512,512,8]{1,0,2:T(8,128)}, f32[512,512,8]{1,0,2:T(8,128)S(1)}, u32[]{:S(2)}) %copy-start.1) | copy-done | bytes 8388632
  81.6 5.6 %fusion.22 = f32[512,512]{0,1:T(8,128)} fusion(f32[512,512]{0,1:T(8,128)} %broadcast_in_dim.18.clone, s32[]{:T(128)S(6)} %select_n.16, bf16[512,8,128]{2,1,0:T(8,128)(2,1)S(1)} %bitcast.163, f32[8,512]{1,0:T(8,128)} %fusion.3, f32[8,512]{1,0:T(8,128)S(1)} %get-tuple-element.69, f32[512,512,8]{1,0,2:T(8,128)} %copy-done.1, pred[512,512]{0,1:T(8,128)(4,1)S(1)} %fusion.27), kind=kOutput, calls=%fused_computation.26 | convolution fusion | flops 547356672 | bytes 9994244 | tf_op jit(solution)/shard_map/kgql,qkgd->lkd/dot_general | solution.py:107
  89.5 3.0 %copy.104 = f32[512,1,8,128]{0,3,2,1:T(8,128)} copy(f32[512,1,8,128]{3,2,0,1:T(8,128)} %bitcast.159) | data formatting | bytes 4194304 | tf_op jit(solution)/shard_map/convert_element_type | solution.py:93
  92.5 6.9 %fusion.11 = f32[512,8]{0,1:T(8,128)S(1)} fusion(f32[512,1,8,128]{0,3,2,1:T(8,128)} %copy.104, bf16[1,1,512,512]{3,2,1,0:T(8,128)(2,1)S(1)} %copy-done.7, s32[]{:T(128)S(6)} %select_n.16, f32[8,512]{1,0:T(8,128)S(1)} %copy-done.12, f32[8,512]{1,0:T(8,128)S(1)} %get-tuple-element.69, f32[512,512,8]{1,0,2:T(8,128)} %copy-done.1, pred[512,512]{0,1:T(8,128)(4,1)S(1)} %fusion.27), kind=kOutput, calls=%fused_computation.17 | convolution fusion | flops 548401152 | bytes 10928132 | tf_op jit(solution)/shard_map/kgql,lkd->qkgd/dot_general | solution.py:90
  99.4 5.5 %fusion.5 = bf16[8,512,512]{1,2,0:T(8,128)(2,1)S(1)} fusion(f32[8,512]{1,0:T(8,128)S(1)} %bitcast.168, f32[8,512]{1,0:T(8,128)S(1)} %copy-done.12, f32[8,512]{1,0:T(8,128)S(1)} %get-tuple-element.69, f32[512,512,8]{1,0,2:T(8,128)} %copy-done.1, pred[512,512]{0,1:T(8,128)(4,1)S(1)} %fusion.27, bf16[512,8,128]{2,1,0:T(8,128)(2,1)S(1)} %bitcast.164, ...), kind=kOutput, calls=%fused_computation.8 | convolution fusion | flops 551550976 | bytes 14073860 | tf_op jit(solution)/shard_map/qkgd,lkd->kgql/dot_general | solution.py:96
  110.2 3.8 %all-to-all-start.3 = ((bf16[128,4,1024]{0,2,1:T(8,128)(2,1)}), bf16[128,4,1024]{0,2,1:T(8,128)(2,1)S(1)}, u32[]{:S(2)}, u32[]{:S(2)}) async-start(bf16[128,4,1024]{0,2,1:T(8,128)(2,1)} %bitcast.161), calls=%async_computation.5 | async-start | bytes 2097152 | tf_op jit(solution)/shard_map/all_to_all | solution.py:161
  116.6 34.8 %reduce-scatter.4.cloned.1.call-done = f32[128,512]{0,1:T(8,128)} async-done(((f32[512,512]{0,1:T(8,128)}), f32[128,512]{0,1:T(8,128)}) %reduce-scatter.4.cloned.1.call-update) | async-done | bytes 262160 | tf_op jit(solution)/shard_map/reduce_scatter | solution.py:157
  155.4 29.2 %all-gather.4.cloned.1.call-done = bf16[512,1024]{0,1:T(8,128)(2,1)} async-done(((bf16[128,1024]{0,1:T(8,128)(2,1)}), bf16[512,1024]{0,1:T(8,128)(2,1)}) %all-gather.4.cloned.1.call-update) | async-done | bytes 1048592 | tf_op jit(solution)/shard_map/all_gather | solution.py:162
  184.5 4.7 %convolution_bitcast_fusion = f32[1024,1024]{0,1:T(8,128)} fusion(bf16[512,1024]{0,1:T(8,128)(2,1)} %all-gather.4.cloned.1.call-done, bf16[512,1024]{1,0:T(8,128)(2,1)} %bitcast.165), kind=kOutput, calls=%fused_computation.14 | convolution fusion | flops 1073741824 | bytes 6291456 | tf_op jit(solution)/shard_map/td,tc->dc/dot_general | solution.py:163
  192.8 4.5 %all-to-all-start.1 = ((bf16[4,128,1024]{2,1,0:T(8,128)(2,1)}), bf16[4,128,1024]{2,1,0:T(8,128)(2,1)}, u32[]{:S(2)}, u32[]{:S(2)}) async-start(bf16[4,128,1024]{2,1,0:T(8,128)(2,1)} %bitcast.30), calls=%async_computation.3 | async-start | bytes 2097152 | tf_op jit(solution)/shard_map/all_to_all | solution.py:169
  197.3 4.4 %multiply_bitcast_fusion.2 = (f32[512,1,8,128]{0,3,2,1:T(8,128)}, f32[512,8,128]{0,2,1:T(8,128)S(1)}) fusion(bf16[8,512,512]{1,2,0:T(8,128)(2,1)} %copy-done.2, bf16[1,1,512,512]{3,2,1,0:T(8,128)(2,1)} %all-gather, s32[]{:T(128)S(6)} %select_n.16), kind=kOutput, calls=%fused_computation.23 | convolution fusion | flops 537395200 | bytes 8519684 | tf_op jit(solution)/shard_map/kgql,lkd->qkgd/dot_general | solution.py:99
  203.5 3.0 %mul.183 = f32[4,128,1024]{1,0,2:T(4,128)} reshape(f32[512,8,128]{0,2,1:T(8,128)} %maximum_multiply_fusion) | data formatting | bytes 4194304 | tf_op jit(solution)/shard_map/mul | solution.py:51
  206.5 2.9 %copy.92 = f32[4,128,1024]{2,1,0:T(8,128)} copy(f32[4,128,1024]{1,0,2:T(4,128)} %mul.183) | data formatting | bytes 4194304 | tf_op jit(solution)/shard_map/mul | solution.py:51
  209.5 3.0 %reshape.284 = f32[4,128,1024]{1,0,2:T(4,128)} reshape(f32[512,1,8,128]{0,3,2,1:T(8,128)} %get-tuple-element.58) | data formatting | bytes 4194304 | tf_op jit(solution)/shard_map/reshape | solution.py:109
  212.5 2.9 %copy.91 = f32[4,128,1024]{2,1,0:T(8,128)} copy(f32[4,128,1024]{1,0,2:T(4,128)} %reshape.284) | data formatting | bytes 4194304 | tf_op jit(solution)/shard_map/reshape | solution.py:109
  219.8 3.5 %add_convert_fusion = bf16[4,128,1024]{2,1,0:T(8,128)(2,1)S(1)} fusion(f32[4,128,1024]{2,1,0:T(8,128)} %copy.92, f32[4,128,1024]{2,1,0:T(8,128)} %copy.91, f32[4,128,1024]{2,1,0:T(8,128)} %mul.178), kind=kLoop, calls=%fused_computation.21 | loop fusion | flops 1572864 | bytes 7340032 | tf_op jit(solution)/shard_map/convert_element_type | solution.py:145
  224.5 4.8 %all-to-all-start.2 = ((bf16[4,128,1024]{1,2,0:T(8,128)(2,1)}), bf16[4,128,1024]{1,2,0:T(8,128)(2,1)S(1)}, u32[]{:S(2)}, u32[]{:S(2)}) async-start(bf16[4,128,1024]{1,2,0:T(8,128)(2,1)} %copy.93), calls=%async_computation.4 | async-start | bytes 2097152 | tf_op jit(solution)/shard_map/all_to_all | solution.py:148
  232.9 21.0 %all-to-all-done.2 = bf16[4,128,1024]{1,2,0:T(8,128)(2,1)S(1)} async-done(((bf16[4,128,1024]{1,2,0:T(8,128)(2,1)}), bf16[4,128,1024]{1,2,0:T(8,128)(2,1)S(1)}, u32[]{:S(2)}, u32[]{:S(2)}) %all-to-all-start.2) | async-done | bytes 1048608 | tf_op jit(solution)/shard_map/all_to_all | solution.py:148
  255.2 3.2 %multiply_bitcast_fusion = f32[1,1024,512]{1,2,0:T(8,128)} fusion(f32[1024,512]{0,1:T(8,128)} %reduce-scatter.8.cloned.1.call-done), kind=kLoop, calls=%fused_computation.20 | loop fusion | flops 524288 | bytes 4194304 | tf_op jit(solution)/shard_map/broadcast_in_dim | solution.py:172
  258.4 2.9 %copy.97 = f32[1,1024,512]{2,1,0:T(8,128)} copy(f32[1,1024,512]{1,2,0:T(8,128)} %multiply_bitcast_fusion) | data formatting | bytes 4194304
  (79 shorter events, 43.3 us)
Async XLA Ops:
  7.2 182.1 %copy-start = (bf16[1,1024,1024]{2,1,0:T(8,128)(2,1)S(1)}, bf16[1,1024,1024]{2,1,0:T(8,128)(2,1)}, u32[]{:S(2)}) copy-start(bf16[1,1024,1024]{2,1,0:T(8,128)(2,1)} %param.23) | copy-start | bytes 6291460
  7.2 11.9 %copy-start.10 = (bf16[1,1,128,512]{3,2,1,0:T(8,128)(2,1)S(1)}, bf16[1,1,128,512]{3,2,1,0:T(8,128)(2,1)}, u32[]{:S(2)}) copy-start(bf16[1,1,128,512]{3,2,1,0:T(8,128)(2,1)} %param.21) | copy-start | bytes 393220
  7.2 46.2 %copy-start.14 = (s32[1,512]{1,0:T(1,128)S(1)}, s32[1,512]{1,0:T(1,128)}, u32[]{:S(2)}) copy-start(s32[1,512]{1,0:T(1,128)} %param.25) | copy-start | bytes 6148
  7.2 46.2 %copy-start.11 = (bf16[1,1,128,512]{3,2,1,0:T(8,128)(2,1)S(1)}, bf16[1,1,128,512]{3,2,1,0:T(8,128)(2,1)}, u32[]{:S(2)}) copy-start(bf16[1,1,128,512]{3,2,1,0:T(8,128)(2,1)} %param.22) | copy-start | bytes 393220
  9.2 60.8 %copy-start.15 = (f32[64]{0:T(128)S(1)}, f32[64]{0:T(128)}, u32[]{:S(2)}) copy-start(f32[64]{0:T(128)} %constant.120) | copy-start | bytes 772
  9.2 62.1 %copy-start.13 = (s32[1,512]{1,0:T(1,128)S(1)}, s32[1,512]{1,0:T(1,128)}, u32[]{:S(2)}) copy-start(s32[1,512]{1,0:T(1,128)} %param.24) | copy-start | bytes 6148
  10.5 69.5 %all-to-all-start = ((bf16[128,4,1024]{2,0,1:T(8,128)(2,1)}), bf16[128,4,1024]{2,0,1:T(8,128)(2,1)S(1)}, u32[]{:S(2)}, u32[]{:S(2)}) async-start(bf16[128,4,1024]{2,0,1:T(8,128)(2,1)} %copy.78), calls=%async_computation | async-start | bytes 2097152 | tf_op jit(solution)/shard_map/all_to_all | solution.py:132
  16.8 98.1 %reduce-scatter.6.cloned.1.call-start = ((), (), s32[]{:S(2)}) async-start(), calls=%async_computation.8 | async-start | bytes 1310720 | tf_op jit(solution)/shard_map/reduce_scatter | solution.py:158
  74.4 3.3 %copy-start.1 = (f32[512,512,8]{1,0,2:T(8,128)}, f32[512,512,8]{1,0,2:T(8,128)S(1)}, u32[]{:S(2)}) copy-start(f32[512,512,8]{1,0,2:T(8,128)S(1)} %get-tuple-element.70) | copy-start | bytes 25165828
  80.3 1.3 copy-start.5
  87.3 64.1 %reduce-scatter.4.cloned.1.call-start = ((), (), s32[]{:S(2)}) async-start(), calls=%async_computation.7 | async-start | bytes 1310720 | tf_op jit(solution)/shard_map/reduce_scatter | solution.py:157
  87.7 4.8 %copy-start.7 = (bf16[1,1,512,512]{3,2,1,0:T(8,128)(2,1)S(1)}, bf16[1,1,512,512]{3,2,1,0:T(8,128)(2,1)}, u32[]{:S(2)}) copy-start(bf16[1,1,512,512]{3,2,1,0:T(8,128)(2,1)} %all-gather.1) | copy-start | bytes 1572868
  87.7 4.8 %copy-start.12 = (f32[8,512]{1,0:T(8,128)S(1)}, f32[8,512]{1,0:T(8,128)}, u32[]{:S(2)}) copy-start(f32[8,512]{1,0:T(8,128)} %fusion.3) | copy-start | bytes 49156
  92.5 6.9 %copy-start.6 = (bf16[64,8,8,128]{3,2,1,0:T(8,128)(2,1)S(1)}, bf16[64,8,8,128]{3,2,1,0:T(8,128)(2,1)}, u32[]{:S(2)}) copy-start(bf16[64,8,8,128]{3,2,1,0:T(8,128)(2,1)} %copy-done.5) | copy-start | bytes 3145732
  99.4 5.5 %copy-start.3 = (bf16[1,1,512,1024]{2,3,1,0:T(8,128)(2,1)S(1)}, bf16[1,1,512,1024]{2,3,1,0:T(8,128)(2,1)}, u32[]{:S(2)}) copy-start(bf16[1,1,512,1024]{2,3,1,0:T(8,128)(2,1)} %copy.108) | copy-start | bytes 3145732
  104.9 2.0 copy-start.2
  104.9 1.6 copy-start.8
  104.9 1.6 copy-start.9
  110.2 43.9 %all-to-all-start.3 = ((bf16[128,4,1024]{0,2,1:T(8,128)(2,1)}), bf16[128,4,1024]{0,2,1:T(8,128)(2,1)S(1)}, u32[]{:S(2)}, u32[]{:S(2)}) async-start(bf16[128,4,1024]{0,2,1:T(8,128)(2,1)} %bitcast.161), calls=%async_computation.5 | async-start | bytes 2097152 | tf_op jit(solution)/shard_map/all_to_all | solution.py:161
  114.0 70.5 %all-gather.4.cloned.1.call-start = ((), (), s32[]{:S(2)}) async-start(), calls=%async_computation.9 | async-start | bytes 1310720 | tf_op jit(solution)/shard_map/all_gather | solution.py:162
  154.0 101.2 %reduce-scatter.8.cloned.1.call-start = ((), (), s32[]{:S(2)}) async-start(), calls=%async_computation.10 | async-start | bytes 6291456 | tf_op jit(solution)/shard_map/reduce_scatter | solution.py:170
  192.8 31.8 %all-to-all-start.1 = ((bf16[4,128,1024]{2,1,0:T(8,128)(2,1)}), bf16[4,128,1024]{2,1,0:T(8,128)(2,1)}, u32[]{:S(2)}, u32[]{:S(2)}) async-start(bf16[4,128,1024]{2,1,0:T(8,128)(2,1)} %bitcast.30), calls=%async_computation.3 | async-start | bytes 2097152 | tf_op jit(solution)/shard_map/all_to_all | solution.py:169
  224.5 29.3 %all-to-all-start.2 = ((bf16[4,128,1024]{1,2,0:T(8,128)(2,1)}), bf16[4,128,1024]{1,2,0:T(8,128)(2,1)S(1)}, u32[]{:S(2)}, u32[]{:S(2)}) async-start(bf16[4,128,1024]{1,2,0:T(8,128)(2,1)} %copy.93), calls=%async_computation.4 | async-start | bytes 2097152 | tf_op jit(solution)/shard_map/all_to_all | solution.py:148
  231.6 23.6 %collective-permute-start = (bf16[128,4096]{1,0:T(8,128)(2,1)}, bf16[128,4096]{1,0:T(8,128)(2,1)}, u32[]{:S(2)}, u32[]{:S(2)}) collective-permute-start(bf16[128,4096]{1,0:T(8,128)(2,1)} %bitcast.56), channel_id=1, source_target_pairs={{8,0},{16,8},{24,16},{9,1},{17,9},{25,17},{10,2},{18,10},{26,18},{... | collective-permute-start | bytes 3145736 | tf_op jit(solution)/shard_map/ppermute | solution.py:16
  (2 other events, 2.2 us)
Sparse Core Ops, SparseCore 0:
  87.4 27.5 reduce-scatter.5
  117.9 33.3 reduce-scatter.3
  154.1 30.3 all-gather.3
  189.4 52.6 reduce-scatter.7
where the time goes:
time: 271 us; the launch traced here: 270 us
  waiting for transfers between devices  85.9 us (32%)
  blocking collectives  50.9 us (19%)
  local copies, waits for them, and re-layouts  47.6 us (18%)
  matrix products  33.6 us (12%)
  starting transfers between devices  20.9 us (8%)
  other arithmetic  17 us (6%)
  between operations  14.1 us (5%)
    reduce_scatter x1, waiting for transfers between devices, on_device(): lax.psum_scatter(key_full, 'ctx', scatter_dimension=0, tiled=True)  34.8 us
    all_gather x1, blocking collectives, on_device(): lax.all_gather(key_row_block, 'ctx', axis=0, tiled=True)  34.3 us
    all_gather x1, waiting for transfers between devices, on_device(): gradient_total = lax.all_gather(kv_grad, 'ctx', axis=0, tiled=True)  29.2 us
    all_to_all x1, waiting for transfers between devices, on_device(): lax.all_to_all(query_back, 'ctx', split_axis=0, concat_axis=1, tiled=True)  21 us
    unnamed x40, local copies, waits for them, and re-layouts  16.7 us
    all_gather x1, blocking collectives, on_device(): lax.all_gather(value_row_block, 'ctx', axis=0, tiled=True)  16.6 us
    mul x4, local copies, waits for them, and re-layouts, rotate_back(): return gradient * cosine + turned * sine_term  10.2 us
    dot_general x1, matrix products, attend_local(): jnp.einsum('kgql,lkd->qkgd', probs_half, v_blk, preferred_element_type=jn...  6.9 us
  transfers between devices with their start and end apart: 9, of which 4 were waited for; matrix products, arithmetic and copies ran while one was open for 25% of the time, Pallas kernels for 0%

commit v1 on v0

--- a/solution.py
+++ b/solution.py
@@ -8,6 +8,12 @@
 QUERY_HEADS = 32
 KEY_VALUE_HEADS = 4
 HEAD_WIDTH = 128
+
+
+def in_order(blocks, dim):
+    dims = list(blocks.shape[1:])
+    dims[dim] *= blocks.shape[0]
+    return jnp.moveaxis(blocks, 0, dim).reshape(dims)
 
 
 def passed_along(value, axis, by):
@@ -159,7 +165,19 @@
     )
     kv_grad = jnp.concatenate([key_sum, value_sum], 1).astype(jnp.bfloat16)
     input_cols = lax.all_to_all(inputs, "ctx", split_axis=1, concat_axis=0, tiled=True)
-    gradient_total = lax.all_gather(kv_grad, "ctx", axis=0, tiled=True)
+    count = lax.axis_size("ctx")
+    pairs_2 = [(i_2, (i_2 + 1) % count) for i_2 in range(count)]
+    back = [(b, a) for a, b in pairs_2]
+    lower, upper = ([], [])
+    for step in range(count - 1):
+        if step % 2 == 0:
+            lower.append(lax.ppermute(lower[-1] if lower else kv_grad, "ctx", pairs_2))
+        else:
+            upper.append(lax.ppermute(upper[-1] if upper else kv_grad, "ctx", back))
+    parts = jnp.stack([*lower[::-1], kv_grad, *upper])
+    shift = lax.axis_index("ctx") - len(lower)
+    parts = parts[(jnp.arange(count) - shift) % count]
+    gradient_total = in_order(parts, 0)
     rows_part = jnp.einsum(
         "td,tc->dc", input_cols, gradient_total, preferred_element_type=jnp.float32
     )

time: 271 us -> 261 us (0.963)
  waiting for transfers between devices: 85.9 us -> 65.3 us
  starting transfers between devices: 20.9 us -> 29.3 us
    all_gather x1 -> x0, waiting for transfers between devices: 29.2 us -> none  [on_device(): gradient_total = lax.all_gather(kv_grad, 'ctx', axis=0, tiled=True)]
    ppermute x0 -> x3, waiting for transfers between devices: none -> 11.3 us  [the longest x2 11.3 us: on_device(): lower.append(lax.ppermute(lower[-1] if lower else kv_grad, 'ctx', pairs_2))]
    ppermute x0 -> x3, starting transfers between devices: none -> 7.59 us  [the longest x2 6.55 us: on_device(): lower.append(lax.ppermute(lower[-1] if lower else kv_grad, 'ctx', pairs_2))]
    unnamed x40 -> x42, local copies, waits for them, and re-layouts: 16.7 us -> 16.6 us
  transfers between devices with their start and end apart: 9 -> 11, of which waited for: 4 -> 4; matrix products, arithmetic and copies ran while one was open for 25% -> 27% of each run, Pallas kernels for 0% -> 0%
where the time goes in v1:
time: 261 us; the launch traced here: 260 us
  waiting for transfers between devices  65.3 us (25%)
  blocking collectives  50.9 us (20%)
  local copies, waits for them, and re-layouts  49.3 us (19%)
  matrix products  33.6 us (13%)
  starting transfers between devices  29.3 us (11%)
  other arithmetic  17.7 us (7%)
  between operations  14.1 us (5%)
    all_gather x1, blocking collectives, on_device(): lax.all_gather(key_row_block, 'ctx', axis=0, tiled=True)  34.3 us
    reduce_scatter x1, waiting for transfers between devices, on_device(): lax.psum_scatter(key_full, 'ctx', scatter_dimension=0, tiled=True)  33.3 us
    all_to_all x1, waiting for transfers between devices, on_device(): lax.all_to_all(query_back, 'ctx', split_axis=0, concat_axis=1, tiled=True)  20.6 us
    all_gather x1, blocking collectives, on_device(): lax.all_gather(value_row_block, 'ctx', axis=0, tiled=True)  16.6 us
    unnamed x42, local copies, waits for them, and re-layouts  16.6 us
    ppermute x2, waiting for transfers between devices, on_device(): lower.append(lax.ppermute(lower[-1] if lower else kv_grad, 'ctx', pairs_2))  11.3 us
    mul x4, local copies, waits for them, and re-layouts, rotate_back(): return gradient * cosine + turned * sine_term  10.1 us
    dot_general x1, matrix products, attend_local(): jnp.einsum('kgql,lkd->qkgd', probs_half, v_blk, preferred_element_type=jn...  6.89 us
  transfers between devices with their start and end apart: 11, of which 4 were waited for; matrix products, arithmetic and copies ran while one was open for 27% of the time, Pallas kernels for 0%

profile of v1, /device:TPU:0, one launch (start us, length us, event | category | flops | bytes accessed | tf_op | source)
XLA Modules:
  0.0 260.2 jit_solution(17814629390102036821)
XLA Ops:
  10.5 6.3 %all-to-all-start = ((bf16[128,4,1024]{2,0,1:T(8,128)(2,1)}), bf16[128,4,1024]{2,0,1:T(8,128)(2,1)S(1)}, u32[]{:S(2)}, u32[]{:S(2)}) async-start(bf16[128,4,1024]{2,0,1:T(8,128)(2,1)} %copy.83), calls=%async_computation | async-start | bytes 2097152 | tf_op jit(solution)/shard_map/all_to_all | solution.py:138
  19.1 34.3 %all-gather = bf16[1,1,512,512]{3,2,1,0:T(8,128)(2,1)} all-gather(bf16[1,1,128,512]{3,2,1,0:T(8,128)(2,1)S(1)} %copy-done.12), channel_id=2, replica_groups=mesh['section'=4,'dp'=2,'ctx'=4] {'ctx'}, dimensions={2}, use_global_device_ids=true | all-gather | bytes 655360 | tf_op jit(solution)/shard_map/all_gather | solution.py:140
  53.4 16.6 %all-gather.1 = bf16[1,1,512,512]{3,2,1,0:T(8,128)(2,1)} all-gather(bf16[1,1,128,512]{3,2,1,0:T(8,128)(2,1)S(1)} %copy-done.13), channel_id=3, replica_groups=mesh['section'=4,'dp'=2,'ctx'=4] {'ctx'}, dimensions={2}, use_global_device_ids=true | all-gather | bytes 655360 | tf_op jit(solution)/shard_map/all_gather | solution.py:141
  74.4 3.3 %copy-done.1 = f32[512,512,8]{1,0,2:T(8,128)} copy-done((f32[512,512,8]{1,0,2:T(8,128)}, f32[512,512,8]{1,0,2:T(8,128)S(1)}, u32[]{:S(2)}) %copy-start.1) | copy-done | bytes 8388632
  81.6 5.4 %fusion.22 = f32[512,512]{1,0:T(8,128)} fusion(f32[512,512]{1,0:T(8,128)} %broadcast_in_dim.18.clone, s32[]{:T(128)S(6)} %select_n.39, bf16[512,8,128]{2,1,0:T(8,128)(2,1)S(1)} %bitcast.174, f32[8,512]{1,0:T(8,128)} %fusion.3, f32[8,512]{1,0:T(8,128)S(1)} %get-tuple-element.67, f32[512,512,8]{1,0,2:T(8,128)} %copy-done.1, pred[512,512]{0,1:T(8,128)(4,1)S(1)} %fusion.28), kind=kOutput, calls=%fused_computation.27 | convolution fusion | flops 547356672 | bytes 9994244 | tf_op jit(solution)/shard_map/kgql,qkgd->lkd/dot_general | solution.py:113
  89.4 3.0 %copy.110 = f32[512,1,8,128]{0,3,2,1:T(8,128)} copy(f32[512,1,8,128]{3,2,0,1:T(8,128)} %bitcast.169) | data formatting | bytes 4194304 | tf_op jit(solution)/shard_map/convert_element_type | solution.py:99
  92.4 6.9 %fusion.11 = f32[512,8]{0,1:T(8,128)S(1)} fusion(f32[512,1,8,128]{0,3,2,1:T(8,128)} %copy.110, bf16[1,1,512,512]{3,2,1,0:T(8,128)(2,1)S(1)} %copy-done.8, s32[]{:T(128)S(6)} %select_n.39, f32[8,512]{1,0:T(8,128)S(1)} %copy-done.14, f32[8,512]{1,0:T(8,128)S(1)} %get-tuple-element.67, f32[512,512,8]{1,0,2:T(8,128)} %copy-done.1, pred[512,512]{0,1:T(8,128)(4,1)S(1)} %fusion.28), kind=kOutput, calls=%fused_computation.18 | convolution fusion | flops 548401152 | bytes 10928132 | tf_op jit(solution)/shard_map/kgql,lkd->qkgd/dot_general | solution.py:96
  99.3 5.5 %fusion.5 = bf16[8,512,512]{1,2,0:T(8,128)(2,1)S(1)} fusion(f32[8,512]{1,0:T(8,128)S(1)} %bitcast.181, f32[8,512]{1,0:T(8,128)S(1)} %copy-done.14, f32[8,512]{1,0:T(8,128)S(1)} %get-tuple-element.67, f32[512,512,8]{1,0,2:T(8,128)} %copy-done.1, pred[512,512]{0,1:T(8,128)(4,1)S(1)} %fusion.28, bf16[512,8,128]{2,1,0:T(8,128)(2,1)S(1)} %bitcast.175, ...), kind=kOutput, calls=%fused_computation.9 | convolution fusion | flops 551550976 | bytes 14073860 | tf_op jit(solution)/shard_map/qkgd,lkd->kgql/dot_general | solution.py:102
  112.6 4.3 %all-to-all-start.3 = ((bf16[128,4,1024]{2,0,1:T(8,128)(2,1)}), bf16[128,4,1024]{2,0,1:T(8,128)(2,1)}, u32[]{:S(2)}, u32[]{:S(2)}) async-start(bf16[128,4,1024]{2,0,1:T(8,128)(2,1)} %copy.100), calls=%async_computation.5 | async-start | bytes 2097152 | tf_op jit(solution)/shard_map/all_to_all | solution.py:167
  117.9 33.3 %reduce-scatter.4.cloned.1.call-done = f32[128,512]{1,0:T(8,128)} async-done(((f32[512,512]{1,0:T(8,128)}), f32[128,512]{1,0:T(8,128)}) %reduce-scatter.4.cloned.1.call-update) | async-done | bytes 262160 | tf_op jit(solution)/shard_map/reduce_scatter | solution.py:163
  156.2 7.2 %collective-permute-done = bf16[128,1024]{1,0:T(8,128)(2,1)S(1)} collective-permute-done((bf16[128,1024]{1,0:T(8,128)(2,1)S(1)}, bf16[128,1024]{1,0:T(8,128)(2,1)S(1)}, u32[]{:S(2)}, u32[]{:S(2)}) %collective-permute-start) | collective-permute-done | bytes 262176 | tf_op jit(solution)/shard_map/ppermute | solution.py:174
  163.3 3.7 %collective-permute-start.1 = (bf16[128,1024]{1,0:T(8,128)(2,1)S(1)}, bf16[128,1024]{1,0:T(8,128)(2,1)S(1)}, u32[]{:S(2)}, u32[]{:S(2)}) collective-permute-start(bf16[128,1024]{1,0:T(8,128)(2,1)S(1)} %collective-permute-done), channel_id=1, source_target_pairs={{0,1},{1,2},{2,3},{3,0},{4,5},{5,6},{6,7},{7,4},{8,9},{9,10},{10,1... | collective-permute-start | bytes 786440 | tf_op jit(solution)/shard_map/ppermute | solution.py:174
  168.9 4.1 %collective-permute-done.1 = bf16[128,1024]{1,0:T(8,128)(2,1)S(1)} collective-permute-done((bf16[128,1024]{1,0:T(8,128)(2,1)S(1)}, bf16[128,1024]{1,0:T(8,128)(2,1)S(1)}, u32[]{:S(2)}, u32[]{:S(2)}) %collective-permute-start.1) | collective-permute-done | bytes 262176 | tf_op jit(solution)/shard_map/ppermute | solution.py:174
  175.7 4.9 %convolution_bitcast_fusion = f32[1024,1024]{0,1:T(8,128)} fusion(bf16[4,128,1024]{2,1,0:T(8,128)(2,1)} %gather_fusion, bf16[128,4,1024]{2,0,1:T(8,128)(2,1)} %all-to-all-done.3), kind=kOutput, calls=%fused_computation.15 | convolution fusion | flops 1073741824 | bytes 6291456 | tf_op jit(solution)/shard_map/td,tc->dc/dot_general | solution.py:181
  182.9 4.5 %all-to-all-start.1 = ((bf16[4,128,1024]{2,1,0:T(8,128)(2,1)}), bf16[4,128,1024]{2,1,0:T(8,128)(2,1)}, u32[]{:S(2)}, u32[]{:S(2)}) async-start(bf16[4,128,1024]{2,1,0:T(8,128)(2,1)} %bitcast.173), calls=%async_computation.3 | async-start | bytes 2097152 | tf_op jit(solution)/shard_map/all_to_all | solution.py:187
  191.8 4.4 %multiply_bitcast_fusion.2 = (f32[512,1,8,128]{0,3,2,1:T(8,128)}, f32[512,8,128]{0,2,1:T(8,128)S(1)}) fusion(bf16[8,512,512]{1,2,0:T(8,128)(2,1)} %copy-done.2, bf16[1,1,512,512]{3,2,1,0:T(8,128)(2,1)} %all-gather, s32[]{:T(128)S(6)} %select_n.39), kind=kOutput, calls=%fused_computation.24 | convolution fusion | flops 537395200 | bytes 8519684 | tf_op jit(solution)/shard_map/kgql,lkd->qkgd/dot_general | solution.py:105
  198.0 3.0 %mul.183 = f32[4,128,1024]{1,0,2:T(4,128)} reshape(f32[512,8,128]{0,2,1:T(8,128)} %maximum_multiply_fusion) | data formatting | bytes 4194304 | tf_op jit(solution)/shard_map/mul | solution.py:57
  201.0 2.9 %copy.97 = f32[4,128,1024]{2,1,0:T(8,128)} copy(f32[4,128,1024]{1,0,2:T(4,128)} %mul.183) | data formatting | bytes 4194304 | tf_op jit(solution)/shard_map/mul | solution.py:57
  203.9 3.0 %reshape.368 = f32[4,128,1024]{1,0,2:T(4,128)} reshape(f32[512,1,8,128]{0,3,2,1:T(8,128)} %get-tuple-element.58) | data formatting | bytes 4194304 | tf_op jit(solution)/shard_map/reshape | solution.py:115
  206.9 3.0 %copy.96 = f32[4,128,1024]{2,1,0:T(8,128)} copy(f32[4,128,1024]{1,0,2:T(4,128)} %reshape.368) | data formatting | bytes 4194304 | tf_op jit(solution)/shard_map/reshape | solution.py:115
  210.0 3.4 %add_convert_fusion = bf16[4,128,1024]{2,1,0:T(8,128)(2,1)S(1)} fusion(f32[4,128,1024]{2,1,0:T(8,128)} %copy.97, f32[4,128,1024]{2,1,0:T(8,128)} %copy.96, f32[4,128,1024]{2,1,0:T(8,128)} %mul.178), kind=kLoop, calls=%fused_computation.22 | loop fusion | flops 1572864 | bytes 7340032 | tf_op jit(solution)/shard_map/convert_element_type | solution.py:151
  214.7 5.1 %all-to-all-start.2 = ((bf16[4,128,1024]{1,2,0:T(8,128)(2,1)}), bf16[4,128,1024]{1,2,0:T(8,128)(2,1)S(1)}, u32[]{:S(2)}, u32[]{:S(2)}) async-start(bf16[4,128,1024]{1,2,0:T(8,128)(2,1)} %copy.98), calls=%async_computation.4 | async-start | bytes 2097152 | tf_op jit(solution)/shard_map/all_to_all | solution.py:154
  223.4 20.6 %all-to-all-done.2 = bf16[4,128,1024]{1,2,0:T(8,128)(2,1)S(1)} async-done(((bf16[4,128,1024]{1,2,0:T(8,128)(2,1)}), bf16[4,128,1024]{1,2,0:T(8,128)(2,1)S(1)}, u32[]{:S(2)}, u32[]{:S(2)}) %all-to-all-start.2) | async-done | bytes 1048608 | tf_op jit(solution)/shard_map/all_to_all | solution.py:154
  245.3 3.2 %multiply_bitcast_fusion = f32[1,1024,512]{1,2,0:T(8,128)} fusion(f32[1024,512]{0,1:T(8,128)} %reduce-scatter.8.cloned.1.call-done), kind=kLoop, calls=%fused_computation.21 | loop fusion | flops 524288 | bytes 4194304 | tf_op jit(solution)/shard_map/broadcast_in_dim | solution.py:190
  (92 shorter events, 54.3 us)
Async XLA Ops:
  7.2 173.5 %copy-start = (bf16[1,1024,1024]{2,1,0:T(8,128)(2,1)S(1)}, bf16[1,1024,1024]{2,1,0:T(8,128)(2,1)}, u32[]{:S(2)}) copy-start(bf16[1,1024,1024]{2,1,0:T(8,128)(2,1)} %param.23) | copy-start | bytes 6291460
  7.2 11.9 %copy-start.12 = (bf16[1,1,128,512]{3,2,1,0:T(8,128)(2,1)S(1)}, bf16[1,1,128,512]{3,2,1,0:T(8,128)(2,1)}, u32[]{:S(2)}) copy-start(bf16[1,1,128,512]{3,2,1,0:T(8,128)(2,1)} %param.21) | copy-start | bytes 393220
  7.2 46.2 %copy-start.13 = (bf16[1,1,128,512]{3,2,1,0:T(8,128)(2,1)S(1)}, bf16[1,1,128,512]{3,2,1,0:T(8,128)(2,1)}, u32[]{:S(2)}) copy-start(bf16[1,1,128,512]{3,2,1,0:T(8,128)(2,1)} %param.22) | copy-start | bytes 393220
  9.2 60.8 %copy-start.16 = (s32[1,512]{1,0:T(1,128)S(1)}, s32[1,512]{1,0:T(1,128)}, u32[]{:S(2)}) copy-start(s32[1,512]{1,0:T(1,128)} %param.25) | copy-start | bytes 6148
  9.2 60.8 %copy-start.17 = (f32[64]{0:T(128)S(1)}, f32[64]{0:T(128)}, u32[]{:S(2)}) copy-start(f32[64]{0:T(128)} %constant.138) | copy-start | bytes 772
  9.2 62.1 %copy-start.15 = (s32[1,512]{1,0:T(1,128)S(1)}, s32[1,512]{1,0:T(1,128)}, u32[]{:S(2)}) copy-start(s32[1,512]{1,0:T(1,128)} %param.24) | copy-start | bytes 6148
  10.5 69.5 %all-to-all-start = ((bf16[128,4,1024]{2,0,1:T(8,128)(2,1)}), bf16[128,4,1024]{2,0,1:T(8,128)(2,1)S(1)}, u32[]{:S(2)}, u32[]{:S(2)}) async-start(bf16[128,4,1024]{2,0,1:T(8,128)(2,1)} %copy.83), calls=%async_computation | async-start | bytes 2097152 | tf_op jit(solution)/shard_map/all_to_all | solution.py:138
  16.8 100.1 %reduce-scatter.6.cloned.1.call-start = ((), (), s32[]{:S(2)}) async-start(), calls=%async_computation.8 | async-start | bytes 1310720 | tf_op jit(solution)/shard_map/reduce_scatter | solution.py:164
  87.1 64.1 %reduce-scatter.4.cloned.1.call-start = ((), (), s32[]{:S(2)}) async-start(), calls=%async_computation.7 | async-start | bytes 1310720 | tf_op jit(solution)/shard_map/reduce_scatter | solution.py:163
  87.6 4.8 %copy-start.8 = (bf16[1,1,512,512]{3,2,1,0:T(8,128)(2,1)S(1)}, bf16[1,1,512,512]{3,2,1,0:T(8,128)(2,1)}, u32[]{:S(2)}) copy-start(bf16[1,1,512,512]{3,2,1,0:T(8,128)(2,1)} %all-gather.1) | copy-start | bytes 1572868
  87.6 4.8 %copy-start.14 = (f32[8,512]{1,0:T(8,128)S(1)}, f32[8,512]{1,0:T(8,128)}, u32[]{:S(2)}) copy-start(f32[8,512]{1,0:T(8,128)} %fusion.3) | copy-start | bytes 49156
  92.3 6.9 %copy-start.7 = (bf16[64,8,8,128]{3,2,1,0:T(8,128)(2,1)S(1)}, bf16[64,8,8,128]{3,2,1,0:T(8,128)(2,1)}, u32[]{:S(2)}) copy-start(bf16[64,8,8,128]{3,2,1,0:T(8,128)(2,1)} %copy-done.6) | copy-start | bytes 3145732
  99.3 7.5 %copy-start.3 = (bf16[1,1,512,1024]{2,3,1,0:T(8,128)(2,1)S(1)}, bf16[1,1,512,1024]{2,3,1,0:T(8,128)(2,1)}, u32[]{:S(2)}) copy-start(bf16[1,1,512,1024]{2,3,1,0:T(8,128)(2,1)} %copy.113) | copy-start | bytes 3145732
  112.6 63.1 %all-to-all-start.3 = ((bf16[128,4,1024]{2,0,1:T(8,128)(2,1)}), bf16[128,4,1024]{2,0,1:T(8,128)(2,1)}, u32[]{:S(2)}, u32[]{:S(2)}) async-start(bf16[128,4,1024]{2,0,1:T(8,128)(2,1)} %copy.100), calls=%async_computation.5 | async-start | bytes 2097152 | tf_op jit(solution)/shard_map/all_to_all | solution.py:167
  116.9 128.5 %reduce-scatter.8.cloned.1.call-start = ((), (), s32[]{:S(2)}) async-start(), calls=%async_computation.9 | async-start | bytes 6291456 | tf_op jit(solution)/shard_map/reduce_scatter | solution.py:188
  152.2 11.1 %collective-permute-start = (bf16[128,1024]{1,0:T(8,128)(2,1)S(1)}, bf16[128,1024]{1,0:T(8,128)(2,1)S(1)}, u32[]{:S(2)}, u32[]{:S(2)}) collective-permute-start(bf16[128,1024]{1,0:T(8,128)(2,1)S(1)} %pad_maximum_fusion.2), channel_id=1, source_target_pairs={{0,1},{1,2},{2,3},{3,0},{4,5},{5,6},{6,7},{7,4},{8,9},{9,10},{10,1... | collective-permute-start | bytes 786440 | tf_op jit(solution)/shard_map/ppermute | solution.py:174
  155.1 13.8 %collective-permute-start.2 = (bf16[128,1024]{1,0:T(8,128)(2,1)S(1)}, bf16[128,1024]{1,0:T(8,128)(2,1)S(1)}, u32[]{:S(2)}, u32[]{:S(2)}) collective-permute-start(bf16[128,1024]{1,0:T(8,128)(2,1)S(1)} %pad_maximum_fusion.2), channel_id=1, source_target_pairs={{1,0},{2,1},{3,2},{0,3},{5,4},{6,5},{7,6},{4,7},{9,8},{10,9},{11,1... | collective-permute-start | bytes 786440 | tf_op jit(solution)/shard_map/ppermute | solution.py:176
  163.3 9.8 %copy-start.11 = (bf16[128,1024]{1,0:T(8,128)(2,1)}, bf16[128,1024]{1,0:T(8,128)(2,1)S(1)}, u32[]{:S(2)}) copy-start(bf16[128,1024]{1,0:T(8,128)(2,1)S(1)} %collective-permute-done) | copy-start | bytes 786436
  163.3 9.8 %collective-permute-start.1 = (bf16[128,1024]{1,0:T(8,128)(2,1)S(1)}, bf16[128,1024]{1,0:T(8,128)(2,1)S(1)}, u32[]{:S(2)}, u32[]{:S(2)}) collective-permute-start(bf16[128,1024]{1,0:T(8,128)(2,1)S(1)} %collective-permute-done), channel_id=1, source_target_pairs={{0,1},{1,2},{2,3},{3,0},{4,5},{5,6},{6,7},{7,4},{8,9},{9,10},{10,1... | collective-permute-start | bytes 786440 | tf_op jit(solution)/shard_map/ppermute | solution.py:174
  175.7 4.9 %copy-start.5 = (bf16[4,128,1024]{2,1,0:T(8,128)(2,1)S(1)}, bf16[4,128,1024]{2,1,0:T(8,128)(2,1)}, u32[]{:S(2)}) copy-start(bf16[4,128,1024]{2,1,0:T(8,128)(2,1)} %gather_fusion) | copy-start | bytes 3145732
  180.6 6.8 %copy-start.9 = (f32[512,64]{0,1:T(8,128)S(1)}, f32[512,64]{0,1:T(8,128)}, u32[]{:S(2)}) copy-start(f32[512,64]{0,1:T(8,128)} %get-tuple-element.64) | copy-start | bytes 393220
  182.9 31.8 %all-to-all-start.1 = ((bf16[4,128,1024]{2,1,0:T(8,128)(2,1)}), bf16[4,128,1024]{2,1,0:T(8,128)(2,1)}, u32[]{:S(2)}, u32[]{:S(2)}) async-start(bf16[4,128,1024]{2,1,0:T(8,128)(2,1)} %bitcast.173), calls=%async_computation.3 | async-start | bytes 2097152 | tf_op jit(solution)/shard_map/all_to_all | solution.py:187
  214.7 29.3 %all-to-all-start.2 = ((bf16[4,128,1024]{1,2,0:T(8,128)(2,1)}), bf16[4,128,1024]{1,2,0:T(8,128)(2,1)S(1)}, u32[]{:S(2)}, u32[]{:S(2)}) async-start(bf16[4,128,1024]{1,2,0:T(8,128)(2,1)} %copy.98), calls=%async_computation.4 | async-start | bytes 2097152 | tf_op jit(solution)/shard_map/all_to_all | solution.py:154
  222.1 23.2 %collective-permute-start.3 = (bf16[128,4096]{1,0:T(8,128)(2,1)}, bf16[128,4096]{1,0:T(8,128)(2,1)}, u32[]{:S(2)}, u32[]{:S(2)}) collective-permute-start(bf16[128,4096]{1,0:T(8,128)(2,1)} %bitcast.64), channel_id=1, source_target_pairs={{8,0},{16,8},{24,16},{9,1},{17,9},{25,17},{10,2},{18,10},{26,18},{... | collective-permute-start | bytes 3145736 | tf_op jit(solution)/shard_map/ppermute | solution.py:22
  (5 other events, 9.1 us)
Sparse Core Ops, SparseCore 0:
  87.2 27.2 reduce-scatter.5
  117.4 33.7 reduce-scatter.3
  180.7 55.1 reduce-scatter.7
